TPU v7x, 128 devices: a whole 4x4x4 slice. The times are simulated.
128 devices in a mesh: gx: 32 (over x, y_lo, z), gy: 4 (over y_hi, core).
Axes of the slice: x: 4, y: 4 (y_hi: 2, y_lo: 2; y = y_hi * 2 + y_lo), z: 4, core: 2. Of those that a mesh axis runs over, the one named last changes fastest.
Arguments:
- pressure: float32 [16, 512, 4096], P(None, 'gy', 'gx'), may hold values from -6 to 6
- vel_x: float32 [16, 512, 4096], P(None, 'gy', 'gx'), may hold values from -3 to 3
- vel_y: float32 [16, 512, 4096], P(None, 'gy', 'gx'), may hold values from -3 to 3
- vel_z: float32 [16, 512, 4096], P(None, 'gy', 'gx'), may hold values from -3 to 3
- memory_one: float32 [16, 512, 4096], P(None, 'gy', 'gx'), may hold values from -6 to 6
- memory_two: float32 [16, 512, 4096], P(None, 'gy', 'gx'), may hold values from -6 to 6
- density: float32 [16, 512, 4096], P(None, 'gy', 'gx'), may hold values from 0.6 to 1.8
- sound_speed: float32 [16, 512, 4096], P(None, 'gy', 'gx'), may hold values from 0.15 to 0.45
- tile_row: int32 [4, 32, 512], P('gy', 'gx'), may hold values from 0 to 2047
- tile_owner: int32 [4, 32, 512, 1], P('gy', 'gx'), may hold values from 0 to 127; in each aligned block of 512 rows (0 to 511, 512 to 1023, ..., all dimensions but the last counted through in order) at most 8 rows name the same one
- src_cell: int32 [4, 32, 256], P('gy', 'gx'), may hold values from 0 to 262143
- src_wave: float32 [4, 32, 4, 256], P('gy', 'gx'), may hold values from -6 to 6
Outputs:
- pressure_out: float32 [16, 512, 4096], P(None, 'gy', 'gx')
- vel_x_out: float32 [16, 512, 4096], P(None, 'gy', 'gx')
- vel_y_out: float32 [16, 512, 4096], P(None, 'gy', 'gx')
- vel_z_out: float32 [16, 512, 4096], P(None, 'gy', 'gx')
- memory_one_out: float32 [16, 512, 4096], P(None, 'gy', 'gx')
- memory_two_out: float32 [16, 512, 4096], P(None, 'gy', 'gx')
- farfield: float32 [2, 16384], P(None, ('gx', 'gy'))
Inputs may be any that keep to these rules, and one draw needn't show every extreme that they name: `tile_owner`: in the tiles of one device, at most 8 have the same owner, and some owner has exactly 8 of them; every device owns some tile.
All inputs are finite; a program needn't handle non-finite values.
Results may differ from a plain program's by a relative error of at most 0.0003.
Values sent between devices are 32-bit elements; how exact they have to be, the bound alone decides.
A program may use at most 128 MiB of HBM per device.

v0:
```python
import functools
import math

import jax
import jax.numpy as jnp
import numpy as np
from jax import lax
from jax.experimental import pallas as pl
from jax.experimental.pallas import tpu as pltpu
from jax.sharding import PartitionSpec as P

MESH = pl.DeviceIdType.MESH
F32 = jnp.float32
BF16 = jnp.bfloat16

ANG = 128
WAVELEN = 16
C1 = 9.0 / 8.0
C2 = 1.0 / 24.0
RELAX1, FEED1 = 0.6, 0.06
RELAX2, FEED2 = 0.9, 0.025
STEP_PHASE = 0.7
IMPEDANCE = 0.35

STEPS = 4
NZ, CY, CX = 16, 128, 128
TILES = 512
SRCS = 256
PAD = 16
ROWS = PAD + CY + 16
CHUNK = 32
NG = 4
GZ = NZ // NG
XOUT = 4
LOW_X, HIGH_X, LOW_Y, HIGH_Y = 0, 1, 2, 3


def split2(value):
    high = value.astype(BF16)
    low = (value - high.astype(F32)).astype(BF16)
    return high, low


def split3(value):
    high = value.astype(BF16)
    rest = value - high.astype(F32)
    mid = rest.astype(BF16)
    low = (rest - mid.astype(F32)).astype(BF16)
    return high, mid, low


def dot(a, b):
    return lax.dot_general(a, b, (((1,), (0,)), ((), ())), preferred_element_type=F32)


def dot_nt(a, b):
    return lax.dot_general(a, b, (((1,), (1,)), ((), ())), preferred_element_type=F32)


def sincos_turns(turns):
    f = turns - jnp.floor(turns + 0.5)
    quad = jnp.floor(f * 4.0 + 0.5)
    x = (f - quad * 0.25) * (2.0 * math.pi)
    x2 = x * x
    s = x * (1.0 + x2 * (-1.0 / 6 + x2 * (1.0 / 120 + x2 * (-1.0 / 5040 + x2 * (1.0 / 362880)))))
    c = 1.0 + x2 * (-0.5 + x2 * (1.0 / 24 + x2 * (-1.0 / 720 + x2 * (1.0 / 40320))))
    swap = jnp.abs(quad) == 1.0
    a = jnp.where(swap, s, c)
    b = jnp.where(swap, c, s)
    cos_sign = jnp.where((quad == 0.0) | (quad == -1.0), 1.0, -1.0)
    sin_sign = jnp.where((quad == 0.0) | (quad == 1.0), 1.0, -1.0)
    return a * cos_sign, b * sin_sign


def unroll_shift(block):
    return (128 - (8 * block + 3)) % 128


def pack_rows(read, group):
    packed = jnp.zeros((8, 128), F32)
    for block in range(16):
        rolled = pltpu.roll(read(block), (8 * block + 3) % 128, 1)
        packed = jnp.where(group == block, rolled, packed)
    return packed


def kernel(
    nx,
    ny,
    p_in,
    vx_in,
    vy_in,
    vz_in,
    m1_in,
    m2_in,
    de_in,
    cs_in,
    row_s,
    row_v,
    own_v,
    cell_v,
    wave_v,
    thi,
    tlo,
    p_out,
    vx_out,
    vy_out,
    vz_out,
    m1_out,
    m2_out,
    ff_out,
    P_,
    VX,
    VY,
    VZ,
    M1,
    M2,
    B,
    MOD,
    CS,
    SRC,
    PO,
    PH,
    XO,
    XH,
    TAB,
    HOT,
    G,
    RA,
    RB,
    RC,
    ld_sem,
    st_sem,
    snd,
    rcv,
    snd0,
    rcv0,
    sa,
    ra,
    sb,
    rb,
    sc,
    rc,
):
    gx = lax.axis_index("gx")
    gy = lax.axis_index("gy")
    devices = nx * ny
    period = 2 * WAVELEN * max(ANG, devices)
    inner = nx // XOUT
    xo, xi = gx // inner, gx % inner
    has = [gx > 0, gx < nx - 1, gy > 0, gy < ny - 1]
    peer = [{"gx": gx - 1}, {"gx": gx + 1}, {"gy": gy - 1}, {"gy": gy + 1}]
    peers_a = [{"gy": (gy + k) % ny} for k in range(1, ny)]
    peers_b = [{"gx": (xo + k) % XOUT * inner + xi} for k in range(1, XOUT)]
    peers_c = [{"gx": xo * inner + (xi + k) % inner} for k in range(1, inner)]

    dst = [
        P_.at[0, pl.ds(1, NZ), pl.ds(PAD, CY), :],
        VX,
        VY.at[:, pl.ds(PAD, CY), :],
        VZ.at[0, pl.ds(2, NZ)],
        M1,
        M2,
        B.at[:, pl.ds(PAD, CY), :],
        CS,
    ]
    src = [p_in, vx_in, vy_in, vz_in, m1_in, m2_in, de_in, cs_in]
    loads = [pltpu.make_async_copy(src[i], dst[i], ld_sem.at[i]) for i in range(8)]
    for i in (0, 1, 6, 7, 2, 3, 4, 5):
        loads[i].start()

    barrier = pltpu.get_barrier_semaphore()
    for d in range(4):

        @pl.when(has[d])
        def _():
            pl.semaphore_signal(barrier, inc=1, device_id=peer[d], device_id_type=MESH)

    for target in peers_a + peers_b + peers_c:
        pl.semaphore_signal(barrier, inc=1, device_id=target, device_id_type=MESH)
    fixed = len(peers_a) + len(peers_b) + len(peers_c)
    neighbours = sum(jnp.where(flag, 1, 0) for flag in has)
    pl.semaphore_wait(barrier, fixed + neighbours)

    lane = lax.broadcasted_iota(jnp.int32, (8, 128), 1)
    group = lane >> 3
    from_low = (lane & 7) < 3

    def rim_copy(s, g, d):
        z0 = g * GZ
        if d in (LOW_X, HIGH_X):
            source = PO.at[s, pl.ds(z0, GZ)]
            target = PH.at[s, HIGH_X if d == LOW_X else LOW_X, pl.ds(z0, GZ)]
        else:
            y_from, y_to = (PAD, PAD + CY) if d == LOW_Y else (PAD + CY - 8, PAD - 8)
            source = P_.at[s, pl.ds(z0 + 1, GZ), pl.ds(y_from, 8), :]
            target = P_.at[s, pl.ds(z0 + 1, GZ), pl.ds(y_to, 8), :]
        back = {LOW_X: HIGH_X, HIGH_X: LOW_X, LOW_Y: HIGH_Y, HIGH_Y: LOW_Y}[d]
        return pltpu.make_async_remote_copy(
            src_ref=source,
            dst_ref=target,
            send_sem=snd.at[s, g, d],
            recv_sem=rcv.at[s, g, back],
            device_id=peer[d],
            device_id_type=MESH,
        )

    def send_rims(s, g):
        for d in range(4):

            @pl.when(has[d])
            def _():
                rim_copy(s, g, d).start()

    def wait_rims(s, g):
        for d in range(4):

            @pl.when(has[d])
            def _():
                back = {LOW_X: HIGH_X, HIGH_X: LOW_X, LOW_Y: HIGH_Y, HIGH_Y: LOW_Y}[d]
                rim_copy(s, g, back).wait_recv()

    def first_copies(d):
        back = {LOW_X: HIGH_X, HIGH_X: LOW_X, LOW_Y: HIGH_Y, HIGH_Y: LOW_Y}[d]
        if d in (LOW_X, HIGH_X):
            pairs = [(XO, XH.at[back])]
        else:
            y_from, y_to = (0, PAD + CY) if d == LOW_Y else (CY - 8, PAD - 8)
            pairs = [
                (vy_in.at[:, pl.ds(y_from, 8), :], VY.at[:, pl.ds(y_to, 8), :]),
                (de_in.at[:, pl.ds(y_from, 8), :], B.at[:, pl.ds(y_to, 8), :]),
            ]
        return [
            pltpu.make_async_remote_copy(
                src_ref=a,
                dst_ref=b,
                send_sem=snd0.at[d, i],
                recv_sem=rcv0.at[back, i],
                device_id=peer[d],
                device_id_type=MESH,
            )
            for i, (a, b) in enumerate(pairs)
        ]

    loads[0].wait()

    def pack_first(z, carry):
        PO[0, z] = pack_rows(lambda k: P_[0, z + 1, PAD + 8 * k : PAD + 8 * k + 8, :], group)
        return carry

    for g in range(NG):
        lax.fori_loop(g * GZ, (g + 1) * GZ, pack_first, 0)
        send_rims(0, g)
    for d in (LOW_Y, HIGH_Y):

        @pl.when(has[d])
        def _():
            for copy in first_copies(d):
                copy.start()

    loads[1].wait()
    loads[6].wait()

    def pack_others(z, carry):
        XO[0, z] = pack_rows(lambda k: VX[z, 8 * k : 8 * k + 8, :], group)
        XO[1, z] = pack_rows(lambda k: B[z, PAD + 8 * k : PAD + 8 * k + 8, :], group)
        return carry

    lax.fori_loop(0, NZ, pack_others, 0)
    for d in (LOW_X, HIGH_X):

        @pl.when(has[d])
        def _():
            for copy in first_copies(d):
                copy.start()

    plane = jnp.zeros((CY, CX), F32)
    for s in range(STEPS):
        for z in (0, NZ + 1, NZ + 2):
            P_[s, z, PAD : PAD + CY, :] = plane
        for z in (0, 1, NZ + 2):
            VZ[s + 1, z] = plane
    rim = jnp.zeros((NZ, 8, 128), F32)
    for d in (LOW_X, HIGH_X):

        @pl.when(jnp.logical_not(has[d]))
        def _():
            for s in range(STEPS):
                PH[s, d] = rim
            XH[d, 0] = rim
            XH[d, 1] = rim + 1.0

    for d, y0 in ((LOW_Y, PAD - 8), (HIGH_Y, PAD + CY)):

        @pl.when(jnp.logical_not(has[d]))
        def _():
            for s in range(STEPS):
                P_[s, 1 : NZ + 1, y0 : y0 + 8, :] = rim
            VY[:, y0 : y0 + 8, :] = rim

    cells = cell_v[...]
    src_row = cells >> 7
    src_lane = cells & 127
    lane_hot = lax.broadcasted_iota(jnp.int32, (CX, SRCS), 0) == src_lane
    parts = []
    for s in range(STEPS):
        parts.append(split3(jnp.where(lane_hot, wave_v[s : s + 1, :], 0.0)))
    right = [jnp.concatenate([parts[s][i] for s in range(STEPS)], axis=0) for i in range(3)]
    for i in range(3):
        HOT[i] = right[i]

    def sources(z, carry):
        rows = lax.broadcasted_iota(jnp.int32, (CY, SRCS), 0) + z * CY
        hot = jnp.where(rows == src_row, 1.0, 0.0).astype(BF16)
        total = dot_nt(hot, HOT[0]) + dot_nt(hot, HOT[1]) + dot_nt(hot, HOT[2])
        for s in range(STEPS):
            SRC[s, z] = total[:, s * CX : (s + 1) * CX]
        return carry

    lax.fori_loop(0, NZ, sources, 0)

    scale = 2.0 * math.pi / period
    magnitude = 2.0 * math.pi / WAVELEN
    angle = lax.broadcasted_iota(jnp.int32, (128, ANG), 1)
    wave_x = (2 * angle + 1 - ANG).astype(F32)
    x_turn = wave_x * (gx * CX).astype(F32)
    kx2 = (scale * wave_x) * (scale * wave_x)
    for k in range(TILES // 128):
        own = jnp.broadcast_to(own_v[:, k * 128 : (k + 1) * 128].astype(F32), (128, 128)).T
        row = jnp.broadcast_to(row_v[:, k * 128 : (k + 1) * 128].astype(F32), (128, 128)).T
        layer = jnp.floor(row * (1.0 / CY))
        tile_y = row - layer * CY + (gy * CY).astype(F32)
        wave_y = 2.0 * own + (1.0 - devices)
        ky = scale * wave_y
        wave_z = jnp.sqrt(magnitude * magnitude - kx2 - ky * ky)
        whole = (x_turn + wave_y * tile_y) * (1.0 / period)
        turns = (whole - jnp.floor(whole)) + wave_z * layer * (1.0 / (2.0 * math.pi))
        cosine, sine = sincos_turns(turns)
        TAB[0, k * 128 : (k + 1) * 128, :] = cosine
        TAB[1, k * 128 : (k + 1) * 128, :] = sine
        TAB[2, k * 128 : (k + 1) * 128, :] = wave_z * (1.0 / magnitude)

    for i in (7, 2, 3, 4, 5):
        loads[i].wait()
    for d in range(4):

        @pl.when(has[d])
        def _():
            back = {LOW_X: HIGH_X, HIGH_X: LOW_X, LOW_Y: HIGH_Y, HIGH_Y: LOW_Y}[d]
            for copy in first_copies(back):
                copy.wait_recv()

    low_ok = jnp.where(has[LOW_X], 1.0, 0.0)
    high_ok = jnp.where(has[HIGH_X], 1.0, 0.0)

    def material(z, carry):
        for y0 in range(0, CY, CHUNK):
            rho = B[z, PAD + y0 : PAD + y0 + CHUNK, :]
            speed = CS[z, y0 : y0 + CHUNK, :]
            MOD[z, y0 : y0 + CHUNK, :] = rho * speed * speed
            B[z, PAD + y0 : PAD + y0 + CHUNK, :] = 1.0 / rho
        XO[0, z] = jnp.where(from_low, XH[LOW_X, 0, z], XH[HIGH_X, 0, z])
        XO[1, z] = jnp.where(
            from_low, low_ok / XH[LOW_X, 1, z], high_ok / XH[HIGH_X, 1, z]
        )
        return carry

    for d in (LOW_X, HIGH_X):

        @pl.when(has[d])
        def _():
            for copy in first_copies(d):
                copy.wait_send()

    lax.fori_loop(0, NZ, material, 0)
    for d, y0 in ((LOW_Y, PAD - 8), (HIGH_Y, PAD + CY)):

        @pl.when(has[d])
        def _():
            B[:, y0 : y0 + 8, :] = 1.0 / B[:, y0 : y0 + 8, :]

        @pl.when(jnp.logical_not(has[d]))
        def _():
            B[:, y0 : y0 + 8, :] = rim

    wide = lax.broadcasted_iota(jnp.int32, (CHUNK, 128), 1)

    def velocities(s, z):
        near = jnp.where(from_low, PH[s, LOW_X, z], PH[s, HIGH_X, z])
        mine = PO[s, z]
        low = jnp.where(from_low, near, mine)
        high = jnp.where(from_low, mine, near)

        def along(v):
            return C1 * (pltpu.roll(v, 127, 1) - v) - C2 * (
                pltpu.roll(v, 126, 1) - pltpu.roll(v, 1, 1)
            )

        XO[0, z] = XO[0, z] - XO[1, z] * jnp.where(from_low, along(low), along(high))
        for y0 in (PAD - 8, PAD + CY):
            f = C1 * (P_[s, z + 1, y0 + 1 : y0 + 9, :] - P_[s, z + 1, y0 : y0 + 8, :]) - C2 * (
                P_[s, z + 1, y0 + 2 : y0 + 10, :] - P_[s, z + 1, y0 - 1 : y0 + 7, :]
            )
            VY[z, y0 : y0 + 8, :] = VY[z, y0 : y0 + 8, :] - B[z, y0 : y0 + 8, :] * f
        for y0 in range(0, CY, CHUNK):
            r = PAD + y0
            e = r + CHUNK
            p = P_[s, z + 1, r:e, :]
            b = B[z, r:e, :]
            halo = jnp.concatenate(
                [pltpu.roll(near, unroll_shift(y0 // 8 + i), 1) for i in range(CHUNK // 8)], axis=0
            )
            left = jnp.where(wide == 127, halo, p)
            next_ = jnp.where(wide == 0, halo, p)
            after = jnp.where(wide < 2, halo, p)
            f = C1 * (pltpu.roll(next_, 127, 1) - p) - C2 * (
                pltpu.roll(after, 126, 1) - pltpu.roll(left, 1, 1)
            )
            VX[z, y0 : y0 + CHUNK, :] = VX[z, y0 : y0 + CHUNK, :] - b * f
            f = C1 * (P_[s, z + 1, r + 1 : e + 1, :] - p) - C2 * (
                P_[s, z + 1, r + 2 : e + 2, :] - P_[s, z + 1, r - 1 : e - 1, :]
            )
            VY[z, r:e, :] = VY[z, r:e, :] - b * f
            f = C1 * (P_[s, z + 2, r:e, :] - p) - C2 * (P_[s, z + 3, r:e, :] - P_[s, z, r:e, :])
            VZ[s + 1, z + 2, y0 : y0 + CHUNK, :] = VZ[s, z + 2, y0 : y0 + CHUNK, :] - b * f

    def pressures(s, z):
        near = XO[0, z]
        packed = jnp.zeros((8, 128), F32)
        for y0 in range(0, CY, CHUNK):
            r = PAD + y0
            e = r + CHUNK
            halo = jnp.concatenate(
                [pltpu.roll(near, unroll_shift(y0 // 8 + i), 1) for i in range(CHUNK // 8)], axis=0
            )
            v = VX[z, y0 : y0 + CHUNK, :]
            left = jnp.where(wide == 127, halo, v)
            before = jnp.where(wide >= 126, halo, v)
            next_ = jnp.where(wide == 0, halo, v)
            div = C1 * (v - pltpu.roll(left, 1, 1)) - C2 * (
                pltpu.roll(next_, 127, 1) - pltpu.roll(before, 2, 1)
            )
            div = div + (
                C1 * (VY[z, r:e, :] - VY[z, r - 1 : e - 1, :])
                - C2 * (VY[z, r + 1 : e + 1, :] - VY[z, r - 2 : e - 2, :])
            )
            q, t = y0, y0 + CHUNK
            div = div + (
                C1 * (VZ[s + 1, z + 2, q:t, :] - VZ[s + 1, z + 1, q:t, :])
                - C2 * (VZ[s + 1, z + 3, q:t, :] - VZ[s + 1, z, q:t, :])
            )
            one = RELAX1 * M1[z, q:t, :] + FEED1 * div
            two = RELAX2 * M2[z, q:t, :] + FEED2 * div
            M1[z, q:t, :] = one
            M2[z, q:t, :] = two
            new = P_[s, z + 1, r:e, :] - MOD[z, q:t, :] * (div - one - two) + SRC[s, z, q:t, :]
            P_[s + 1, z + 1, r:e, :] = new
            for i in range(CHUNK // 8):
                block = y0 // 8 + i
                rolled = pltpu.roll(new[8 * i : 8 * i + 8, :], (8 * block + 3) % 128, 1)
                packed = jnp.where(group == block, rolled, packed)
        PO[s + 1, z] = packed

    def stores(g):
        zs = pl.ds(g * GZ, GZ)
        pairs = [
            (P_.at[STEPS, pl.ds(g * GZ + 1, GZ), pl.ds(PAD, CY), :], p_out.at[zs]),
            (VX.at[zs], vx_out.at[zs]),
            (VY.at[zs, pl.ds(PAD, CY), :], vy_out.at[zs]),
            (VZ.at[STEPS, pl.ds(g * GZ + 2, GZ)], vz_out.at[zs]),
            (M1.at[zs], m1_out.at[zs]),
            (M2.at[zs], m2_out.at[zs]),
        ]
        return [pltpu.make_async_copy(a, b, st_sem.at[g, i]) for i, (a, b) in enumerate(pairs)]

    def step(s, carry):
        def planes(z, inner_carry):
            @pl.when(z < NZ)
            def _():
                @pl.when(z % GZ == 0)
                def _():
                    wait_rims(s, z // GZ)

                velocities(s, z)

            @pl.when(z > 0)
            def _():
                pressures(s, z - 1)

                @pl.when(z % GZ == 0)
                def _():
                    g = z // GZ - 1

                    @pl.when(s < STEPS - 1)
                    def _():
                        send_rims(s + 1, g)

                    @pl.when(s == STEPS - 1)
                    def _():
                        for copy in stores(g):
                            copy.start()

            return inner_carry

        return lax.fori_loop(0, NZ + 1, planes, carry)

    lax.fori_loop(0, STEPS, step, 0)

    def gather(t, carry):
        r = row_s[t]
        z = r >> 7
        y = r & 127
        for s in range(STEPS):
            G[s, pl.ds(t, 1), :] = P_[s + 1, z + 1, pl.ds(y + PAD, 1), :]
            G[STEPS + s, pl.ds(t, 1), :] = VZ[s + 1, z + 2, pl.ds(y, 1), :]
        return carry

    lax.fori_loop(0, TILES, gather, 0, unroll=8)

    weights = [(math.cos(STEP_PHASE * (s + 1)), math.sin(STEP_PHASE * (s + 1))) for s in range(STEPS)]
    own_row = own_v[...]
    order = (own_row % ny) * nx + own_row // ny
    hot = jnp.where(
        lax.broadcasted_iota(jnp.int32, (devices, TILES), 0) == order, 1.0, 0.0
    ).astype(BF16)
    total = jnp.zeros((devices, 2 * ANG), F32)
    for k in range(TILES // 128):
        t0, t1 = k * 128, (k + 1) * 128

        def mixed(base):
            fields = [G[base + s, t0:t1, :] for s in range(STEPS)]
            real = sum(weights[s][0] * fields[s] for s in range(STEPS))
            imag = sum(weights[s][1] * fields[s] for s in range(STEPS))
            high, low = split2(jnp.concatenate([real, imag], axis=1))
            return dot(high, thi[...]) + dot(low, thi[...]) + dot(high, tlo[...])

        press = mixed(0)
        flow = mixed(STEPS)
        cosine, sine, lift = TAB[0, t0:t1, :], TAB[1, t0:t1, :], TAB[2, t0:t1, :]
        real = lift * press[:, :ANG] + IMPEDANCE * flow[:, :ANG]
        imag = lift * press[:, ANG:] + IMPEDANCE * flow[:, ANG:]
        both = jnp.concatenate([cosine * real + sine * imag, cosine * imag - sine * real], axis=1)
        high, low = split2(both)
        total = total + (dot(hot[:, t0:t1], high) + dot(hot[:, t0:t1], low))
    for j in range(ny):
        RA[ny + j] = total[j * nx : (j + 1) * nx, :]

    def exchange(targets, source_of, slots, send, recv):
        copies = []
        for k, target in enumerate(targets):
            copy = pltpu.make_async_remote_copy(
                src_ref=source_of(k + 1),
                dst_ref=slots.at[k + 1],
                send_sem=send.at[k],
                recv_sem=recv.at[k],
                device_id=target,
                device_id_type=MESH,
            )
            copy.start()
            copies.append(copy)
        return copies

    copies = exchange(peers_a, lambda k: RA.at[ny + (gy + k) % ny], RA, sa, ra)
    part = RA[ny + gy]
    for k, copy in enumerate(copies):
        copy.wait()
        part = part + RA[k + 1]
    for j in range(XOUT):
        RB[XOUT + j] = part[j * inner : (j + 1) * inner, :]
    copies = exchange(peers_b, lambda k: RB.at[XOUT + (xo + k) % XOUT], RB, sb, rb)
    part = RB[XOUT + xo]
    for k, copy in enumerate(copies):
        copy.wait()
        part = part + RB[k + 1]
    RC[0] = part
    copies = exchange(peers_c, lambda k: RC.at[0], RC, sc, rc)
    for k, copy in enumerate(copies):
        copy.wait()
        part = part + RC[k + 1]
    norm = 1.0 / math.sqrt(TILES * CX)
    keep = lax.broadcasted_iota(jnp.int32, (inner, 2 * ANG), 0) == xi
    final = jnp.sum(jnp.where(keep, part, 0.0), axis=0, keepdims=True) * norm
    ff_out[0:1, :] = final[:, :ANG]
    ff_out[1:2, :] = final[:, ANG:]

    def drain(i, carry):
        s, g = i // NG, i % NG
        for d in range(4):

            @pl.when(has[d])
            def _():
                rim_copy(s, g, d).wait_send()

        return carry

    lax.fori_loop(0, STEPS * NG, drain, 0)
    for d in (LOW_Y, HIGH_Y):

        @pl.when(has[d])
        def _():
            for copy in first_copies(d):
                copy.wait_send()

    for g in range(NG):
        for copy in stores(g):
            copy.wait()


def tables():
    period = 4096
    wave = 2 * np.arange(ANG) + 1 - ANG
    phase = 2.0 * np.pi * ((np.arange(CX)[:, None] * wave[None, :]) % period) / period
    c, s = np.cos(phase), np.sin(phase)
    table = np.concatenate(
        [np.concatenate([c, -s], axis=1), np.concatenate([s, c], axis=1)], axis=0
    ).astype(np.float32)
    high = table.astype(jnp.bfloat16)
    low = (table - high.astype(np.float32)).astype(jnp.bfloat16)
    return high, low


def local(nx, ny, *args):
    fields = args[:8]
    tile_row, tile_owner, src_cell, src_wave = args[8:]
    rows = tile_row.reshape(TILES)
    high, low = tables()
    block = jax.ShapeDtypeStruct((NZ, CY, CX), F32)
    anywhere = pl.BlockSpec(memory_space=pl.ANY)
    vmem = pl.BlockSpec(memory_space=pltpu.VMEM)
    smem = pl.BlockSpec(memory_space=pltpu.SMEM)
    dma = pltpu.SemaphoreType.DMA
    inner = nx // XOUT
    return pl.pallas_call(
        functools.partial(kernel, nx, ny),
        out_shape=[block] * 6 + [jax.ShapeDtypeStruct((2, ANG), F32)],
        in_specs=[anywhere] * 8 + [smem] + [vmem] * 6,
        out_specs=[anywhere] * 6 + [vmem],
        scratch_shapes=[
            pltpu.VMEM((STEPS + 1, NZ + 3, ROWS, CX), F32),
            pltpu.VMEM((NZ, CY, CX), F32),
            pltpu.VMEM((NZ, ROWS, CX), F32),
            pltpu.VMEM((STEPS + 1, NZ + 3, CY, CX), F32),
            pltpu.VMEM((NZ, CY, CX), F32),
            pltpu.VMEM((NZ, CY, CX), F32),
            pltpu.VMEM((NZ, ROWS, CX), F32),
            pltpu.VMEM((NZ, CY, CX), F32),
            pltpu.VMEM((NZ, CY, CX), F32),
            pltpu.VMEM((STEPS, NZ, CY, CX), F32),
            pltpu.VMEM((STEPS + 1, NZ, 8, CX), F32),
            pltpu.VMEM((STEPS, 2, NZ, 8, CX), F32),
            pltpu.VMEM((2, NZ, 8, CX), F32),
            pltpu.VMEM((2, 2, NZ, 8, CX), F32),
            pltpu.VMEM((3, TILES, ANG), F32),
            pltpu.VMEM((3, STEPS * CX, SRCS), BF16),
            pltpu.VMEM((2 * STEPS, TILES, CX), F32),
            pltpu.VMEM((2 * ny, nx, 2 * ANG), F32),
            pltpu.VMEM((2 * XOUT, inner, 2 * ANG), F32),
            pltpu.VMEM((inner, inner, 2 * ANG), F32),
            dma((8,)),
            dma((NG, 6)),
            dma((STEPS, NG, 4)),
            dma((STEPS, NG, 4)),
            dma((4, 2)),
            dma((4, 2)),
            dma((ny - 1,)),
            dma((ny - 1,)),
            dma((XOUT - 1,)),
            dma((XOUT - 1,)),
            dma((inner - 1,)),
            dma((inner - 1,)),
        ],
        compiler_params=pltpu.CompilerParams(
            collective_id=0, has_side_effects=True, vmem_limit_bytes=56 * 1024 * 1024
        ),
    )(
        *fields,
        rows,
        rows.reshape(1, TILES),
        tile_owner.reshape(1, TILES),
        src_cell.reshape(1, SRCS),
        src_wave.reshape(STEPS, SRCS),
        high,
        low,
    )


def solution(mesh):
    field = P(None, "gy", "gx")
    return jax.shard_map(
        functools.partial(local, mesh.shape["gx"], mesh.shape["gy"]),
        mesh=mesh,
        in_specs=(field,) * 8
        + (
            P("gy", "gx", None),
            P("gy", "gx", None, None),
            P("gy", "gx", None),
            P("gy", "gx", None, None),
        ),
        out_specs=(field,) * 6 + (P(None, ("gx", "gy")),),
        check_vma=False,
    )
```

profile of v0, /device:TPU:1, one launch (start us, length us, event | category | flops | bytes accessed | tf_op | source)
XLA Modules:
  0.0 77.0 jit_solution(14296170325390112171)
XLA Ops:
  0.6 66.0 %shard_map.189 = (f32[16,128,128]{2,1,0:T(8,128)}, f32[16,128,128]{2,1,0:T(8,128)}, f32[16,128,128]{2,1,0:T(8,128)}, f32[16,128,128]{2,1,0:T(8,128)}, f32[16,128...) custom-call(f32[16,128,128]{2,1,0:T(8,128)} %p_in.1, f32[16,128,128]{2,1,0:T(8,128)} %vx_in.1, ...), custom_call_target="tpu_custom_call" | custom-call | tf_op jit(solution)/shard_map/pallas_call | solution.py:633
  66.6 0.0 copy-start.4
  66.6 2.4 %copy.28 = f32[16,128,128]{2,1,0:T(8,128)} copy(f32[16,128,128]{2,1,0:T(8,128)} %get-tuple-element.14) | data formatting | bytes 2097152
  69.0 0.0 copy-done.4
  69.0 0.0 copy-start.3
  69.0 1.0 %copy.29 = f32[16,128,128]{2,1,0:T(8,128)} copy(f32[16,128,128]{2,1,0:T(8,128)S(1)} %copy-done.4) | data formatting | bytes 2097152
  70.0 0.6 copy-done.3
  70.6 0.0 copy-start.2
  70.6 1.0 %copy.30 = f32[16,128,128]{2,1,0:T(8,128)} copy(f32[16,128,128]{2,1,0:T(8,128)S(1)} %copy-done.3) | data formatting | bytes 2097152
  71.6 0.6 copy-done.2
  72.2 0.0 copy-start.1
  72.2 1.0 %copy.31 = f32[16,128,128]{2,1,0:T(8,128)} copy(f32[16,128,128]{2,1,0:T(8,128)S(1)} %copy-done.2) | data formatting | bytes 2097152
  73.2 0.6 copy-done.1
  73.8 0.0 copy-start
  73.8 1.0 %copy.32 = f32[16,128,128]{2,1,0:T(8,128)} copy(f32[16,128,128]{2,1,0:T(8,128)S(1)} %copy-done.1) | data formatting | bytes 2097152
  74.8 0.6 copy-done
  75.4 0.0 copy-start.5
  75.4 1.0 %copy.33 = f32[16,128,128]{2,1,0:T(8,128)} copy(f32[16,128,128]{2,1,0:T(8,128)S(1)} %copy-done) | data formatting | bytes 2097152
  76.4 0.0 copy-done.5
  76.4 0.6 copy.34
Async XLA Ops:
  66.6 2.4 %copy-start.4 = (f32[16,128,128]{2,1,0:T(8,128)S(1)}, f32[16,128,128]{2,1,0:T(8,128)}, u32[]{:S(2)}) copy-start(f32[16,128,128]{2,1,0:T(8,128)} %get-tuple-element.15) | copy-start | bytes 3145732
  69.0 1.6 %copy-start.3 = (f32[16,128,128]{2,1,0:T(8,128)S(1)}, f32[16,128,128]{2,1,0:T(8,128)}, u32[]{:S(2)}) copy-start(f32[16,128,128]{2,1,0:T(8,128)} %get-tuple-element.16) | copy-start | bytes 3145732
  70.6 1.6 %copy-start.2 = (f32[16,128,128]{2,1,0:T(8,128)S(1)}, f32[16,128,128]{2,1,0:T(8,128)}, u32[]{:S(2)}) copy-start(f32[16,128,128]{2,1,0:T(8,128)} %get-tuple-element.17) | copy-start | bytes 3145732
  72.2 1.6 %copy-start.1 = (f32[16,128,128]{2,1,0:T(8,128)S(1)}, f32[16,128,128]{2,1,0:T(8,128)}, u32[]{:S(2)}) copy-start(f32[16,128,128]{2,1,0:T(8,128)} %get-tuple-element.18) | copy-start | bytes 3145732
  73.8 1.6 %copy-start = (f32[16,128,128]{2,1,0:T(8,128)S(1)}, f32[16,128,128]{2,1,0:T(8,128)}, u32[]{:S(2)}) copy-start(f32[16,128,128]{2,1,0:T(8,128)} %get-tuple-element.19) | copy-start | bytes 3145732
  75.4 1.0 %copy-start.5 = (f32[2,128]{1,0:T(2,128)S(1)}, f32[2,128]{1,0:T(2,128)}, u32[]{:S(2)}) copy-start(f32[2,128]{1,0:T(2,128)} %get-tuple-element.20) | copy-start | bytes 3076
where the time goes:
time: 78 us; the launch traced here: 77 us
  Pallas kernels  66 us (85%)
  local copies, waits for them, and re-layouts  10.3 us (13%)
    pallas_call x1, Pallas kernels, local(): pl.pallas_call(functools.partial(kernel, nx, ny), out_shape=[block] * 6 +...  66 us
    unnamed x19, local copies, waits for them, and re-layouts  10.3 us

commit v1 on v0

--- a/solution.py
+++ b/solution.py
@@ -15,8 +15,8 @@
 
 ANG = 128
 WAVELEN = 16
-C1 = 9.0 / 8.0
-C2 = 1.0 / 24.0
+UNIT = 1.0 / 24.0
+NEAR = 27.0
 RELAX1, FEED1 = 0.6, 0.06
 RELAX2, FEED2 = 0.9, 0.025
 STEP_PHASE = 0.7
@@ -31,6 +31,7 @@
 CHUNK = 32
 NG = 4
 GZ = NZ // NG
+PB = 4
 XOUT = 4
 LOW_X, HIGH_X, LOW_Y, HIGH_Y = 0, 1, 2, 3
 
@@ -70,10 +71,6 @@
     cos_sign = jnp.where((quad == 0.0) | (quad == -1.0), 1.0, -1.0)
     sin_sign = jnp.where((quad == 0.0) | (quad == 1.0), 1.0, -1.0)
     return a * cos_sign, b * sin_sign
-
-
-def unroll_shift(block):
-    return (128 - (8 * block + 3)) % 128
 
 
 def pack_rows(read, group):
@@ -102,19 +99,18 @@
     wave_v,
     thi,
     tlo,
+    wp,
+    wv,
     p_out,
-    vx_out,
+    VX,
     vy_out,
     vz_out,
-    m1_out,
-    m2_out,
+    M1,
+    M2,
     ff_out,
     P_,
-    VX,
     VY,
     VZ,
-    M1,
-    M2,
     B,
     MOD,
     CS,
@@ -122,12 +118,14 @@
     PO,
     PH,
     XO,
+    XM,
     XH,
     TAB,
     HOT,
+    HP,
+    HV,
     G,
     RA,
-    RB,
     RC,
     ld_sem,
     st_sem,
@@ -137,8 +135,6 @@
     rcv0,
     sa,
     ra,
-    sb,
-    rb,
     sc,
     rc,
 ):
@@ -147,11 +143,12 @@
     devices = nx * ny
     period = 2 * WAVELEN * max(ANG, devices)
     inner = nx // XOUT
+    outer = ny * XOUT
     xo, xi = gx // inner, gx % inner
     has = [gx > 0, gx < nx - 1, gy > 0, gy < ny - 1]
     peer = [{"gx": gx - 1}, {"gx": gx + 1}, {"gy": gy - 1}, {"gy": gy + 1}]
-    peers_a = [{"gy": (gy + k) % ny} for k in range(1, ny)]
-    peers_b = [{"gx": (xo + k) % XOUT * inner + xi} for k in range(1, XOUT)]
+    offsets = [(a, b) for a in range(ny) for b in range(XOUT)][1:]
+    peers_a = [{"gx": (xo + b) % XOUT * inner + xi, "gy": (gy + a) % ny} for a, b in offsets]
     peers_c = [{"gx": xo * inner + (xi + k) % inner} for k in range(1, inner)]
 
     dst = [
@@ -176,12 +173,9 @@
         def _():
             pl.semaphore_signal(barrier, inc=1, device_id=peer[d], device_id_type=MESH)
 
-    for target in peers_a + peers_b + peers_c:
+    for target in peers_a + peers_c:
         pl.semaphore_signal(barrier, inc=1, device_id=target, device_id_type=MESH)
-    fixed = len(peers_a) + len(peers_b) + len(peers_c)
-    neighbours = sum(jnp.where(flag, 1, 0) for flag in has)
-    pl.semaphore_wait(barrier, fixed + neighbours)
-
+    fixed = len(peers_a) + len(peers_c)
     lane = lax.broadcasted_iota(jnp.int32, (8, 128), 1)
     group = lane >> 3
     from_low = (lane & 7) < 3
@@ -242,38 +236,6 @@
             for i, (a, b) in enumerate(pairs)
         ]
 
-    loads[0].wait()
-
-    def pack_first(z, carry):
-        PO[0, z] = pack_rows(lambda k: P_[0, z + 1, PAD + 8 * k : PAD + 8 * k + 8, :], group)
-        return carry
-
-    for g in range(NG):
-        lax.fori_loop(g * GZ, (g + 1) * GZ, pack_first, 0)
-        send_rims(0, g)
-    for d in (LOW_Y, HIGH_Y):
-
-        @pl.when(has[d])
-        def _():
-            for copy in first_copies(d):
-                copy.start()
-
-    loads[1].wait()
-    loads[6].wait()
-
-    def pack_others(z, carry):
-        XO[0, z] = pack_rows(lambda k: VX[z, 8 * k : 8 * k + 8, :], group)
-        XO[1, z] = pack_rows(lambda k: B[z, PAD + 8 * k : PAD + 8 * k + 8, :], group)
-        return carry
-
-    lax.fori_loop(0, NZ, pack_others, 0)
-    for d in (LOW_X, HIGH_X):
-
-        @pl.when(has[d])
-        def _():
-            for copy in first_copies(d):
-                copy.start()
-
     plane = jnp.zeros((CY, CX), F32)
     for s in range(STEPS):
         for z in (0, NZ + 1, NZ + 2):
@@ -297,27 +259,6 @@
             for s in range(STEPS):
                 P_[s, 1 : NZ + 1, y0 : y0 + 8, :] = rim
             VY[:, y0 : y0 + 8, :] = rim
-
-    cells = cell_v[...]
-    src_row = cells >> 7
-    src_lane = cells & 127
-    lane_hot = lax.broadcasted_iota(jnp.int32, (CX, SRCS), 0) == src_lane
-    parts = []
-    for s in range(STEPS):
-        parts.append(split3(jnp.where(lane_hot, wave_v[s : s + 1, :], 0.0)))
-    right = [jnp.concatenate([parts[s][i] for s in range(STEPS)], axis=0) for i in range(3)]
-    for i in range(3):
-        HOT[i] = right[i]
-
-    def sources(z, carry):
-        rows = lax.broadcasted_iota(jnp.int32, (CY, SRCS), 0) + z * CY
-        hot = jnp.where(rows == src_row, 1.0, 0.0).astype(BF16)
-        total = dot_nt(hot, HOT[0]) + dot_nt(hot, HOT[1]) + dot_nt(hot, HOT[2])
-        for s in range(STEPS):
-            SRC[s, z] = total[:, s * CX : (s + 1) * CX]
-        return carry
-
-    lax.fori_loop(0, NZ, sources, 0)
 
     scale = 2.0 * math.pi / period
     magnitude = 2.0 * math.pi / WAVELEN
@@ -340,6 +281,56 @@
         TAB[1, k * 128 : (k + 1) * 128, :] = sine
         TAB[2, k * 128 : (k + 1) * 128, :] = wave_z * (1.0 / magnitude)
 
+    loads[0].wait()
+
+    def pack_first(z, carry):
+        PO[0, z] = pack_rows(lambda k: P_[0, z + 1, PAD + 8 * k : PAD + 8 * k + 8, :], group)
+        return carry
+
+    lax.fori_loop(0, NZ, pack_first, 0)
+    loads[1].wait()
+    loads[6].wait()
+
+    def pack_others(z, carry):
+        XO[0, z] = pack_rows(lambda k: VX[z, 8 * k : 8 * k + 8, :], group)
+        XO[1, z] = pack_rows(lambda k: B[z, PAD + 8 * k : PAD + 8 * k + 8, :], group)
+        return carry
+
+    lax.fori_loop(0, NZ, pack_others, 0)
+
+    neighbours = sum(jnp.where(flag, 1, 0) for flag in has)
+    pl.semaphore_wait(barrier, fixed + neighbours)
+    for d in range(4):
+
+        @pl.when(has[d])
+        def _():
+            for copy in first_copies(d):
+                copy.start()
+
+    for g in range(NG):
+        send_rims(0, g)
+
+    cells = cell_v[...]
+    src_row = cells >> 7
+    src_lane = cells & 127
+    lane_hot = lax.broadcasted_iota(jnp.int32, (CX, SRCS), 0) == src_lane
+    parts = []
+    for s in range(STEPS):
+        parts.append(split3(jnp.where(lane_hot, wave_v[s : s + 1, :], 0.0)))
+    right = [jnp.concatenate([parts[s][i] for s in range(STEPS)], axis=0) for i in range(3)]
+    for i in range(3):
+        HOT[i] = right[i]
+
+    def sources(z, carry):
+        rows = lax.broadcasted_iota(jnp.int32, (CY, SRCS), 0) + z * CY
+        hot = jnp.where(rows == src_row, 1.0, 0.0).astype(BF16)
+        total = dot_nt(hot, HOT[0]) + dot_nt(hot, HOT[1]) + dot_nt(hot, HOT[2])
+        for s in range(STEPS):
+            SRC[s, z] = total[:, s * CX : (s + 1) * CX]
+        return carry
+
+    lax.fori_loop(0, NZ, sources, 0)
+
     for i in (7, 2, 3, 4, 5):
         loads[i].wait()
     for d in range(4):
@@ -350,15 +341,17 @@
             for copy in first_copies(back):
                 copy.wait_recv()
 
-    low_ok = jnp.where(has[LOW_X], 1.0, 0.0)
-    high_ok = jnp.where(has[HIGH_X], 1.0, 0.0)
+    low_ok = jnp.where(has[LOW_X], UNIT, 0.0)
+    high_ok = jnp.where(has[HIGH_X], UNIT, 0.0)
 
     def material(z, carry):
         for y0 in range(0, CY, CHUNK):
             rho = B[z, PAD + y0 : PAD + y0 + CHUNK, :]
             speed = CS[z, y0 : y0 + CHUNK, :]
             MOD[z, y0 : y0 + CHUNK, :] = rho * speed * speed
-            B[z, PAD + y0 : PAD + y0 + CHUNK, :] = 1.0 / rho
+            B[z, PAD + y0 : PAD + y0 + CHUNK, :] = UNIT / rho
+        XM[0, z] = XO[0, z]
+        XM[1, z] = UNIT / XO[1, z]
         XO[0, z] = jnp.where(from_low, XH[LOW_X, 0, z], XH[HIGH_X, 0, z])
         XO[1, z] = jnp.where(
             from_low, low_ok / XH[LOW_X, 1, z], high_ok / XH[HIGH_X, 1, z]
@@ -377,119 +370,132 @@
 
         @pl.when(has[d])
         def _():
-            B[:, y0 : y0 + 8, :] = 1.0 / B[:, y0 : y0 + 8, :]
+            B[:, y0 : y0 + 8, :] = UNIT / B[:, y0 : y0 + 8, :]
 
         @pl.when(jnp.logical_not(has[d]))
         def _():
             B[:, y0 : y0 + 8, :] = rim
 
-    wide = lax.broadcasted_iota(jnp.int32, (CHUNK, 128), 1)
-
-    def velocities(s, z):
-        near = jnp.where(from_low, PH[s, LOW_X, z], PH[s, HIGH_X, z])
-        mine = PO[s, z]
-        low = jnp.where(from_low, near, mine)
-        high = jnp.where(from_low, mine, near)
+    def corrected(change, first, second, weights):
+        high = change.astype(BF16).astype(F32)
+        rest = change - high
+        mid = rest.astype(BF16).astype(F32)
+        low = (rest - mid).astype(BF16).astype(F32)
+        terms = jnp.where(first, high, jnp.where(second, pltpu.roll(mid, 3, 1), pltpu.roll(low, 126, 1)))
+        left = [
+            jnp.where(group == block, terms[8 * i : 8 * i + 8, :], 0.0)
+            for i in range(PB)
+            for block in range(CY // 8)
+        ]
+        fixed = dot(jnp.concatenate(left, axis=0).astype(BF16), weights)
+        return fixed.reshape(PB, CY, CX)
+
+    places = lax.broadcasted_iota(jnp.int32, (8 * PB, 128), 1) & 7
+    lows = places < 3
+
+    def rims(s, k):
+        zs = pl.ds(k * PB, PB)
+
+        def flat(v):
+            return v.reshape(8 * PB, 128)
+
+        near = jnp.where(lows, flat(PH[s, LOW_X, zs]), flat(PH[s, HIGH_X, zs]))
+        mine = flat(PO[s, zs])
+        low = jnp.where(lows, near, mine)
+        high = jnp.where(lows, mine, near)
 
         def along(v):
-            return C1 * (pltpu.roll(v, 127, 1) - v) - C2 * (
-                pltpu.roll(v, 126, 1) - pltpu.roll(v, 1, 1)
+            return NEAR * (pltpu.roll(v, 127, 1) - v) - (pltpu.roll(v, 126, 1) - pltpu.roll(v, 1, 1))
+
+        along_low, along_high = along(low), along(high)
+        theirs = flat(XO[0, zs]) - flat(XO[1, zs]) * jnp.where(lows, along_low, along_high)
+        own = flat(XM[0, zs]) - flat(XM[1, zs]) * jnp.where(lows, along_high, along_low)
+        XO[0, zs] = theirs.reshape(PB, 8, 128)
+        XM[0, zs] = own.reshape(PB, 8, 128)
+        HP[...] = corrected(near - mine, (places >= 2) & (places <= 4), places >= 5, wp[...])
+        HV[k % 2] = corrected(theirs - own, (places >= 1) & (places <= 3), places >= 4, wv[...])
+
+    def velocities(s, k):
+        z = k * PB
+
+        def at(dz, y0, y1):
+            return P_[s, pl.ds(z + 1 + dz, PB), y0:y1, :]
+
+        zs = pl.ds(z, PB)
+        r, e = PAD, PAD + CY
+        p = at(0, r, e)
+        b = B[zs, r:e, :]
+        fz = NEAR * (at(1, r, e) - p) - (at(2, r, e) - at(-1, r, e))
+        new_z = VZ[s, pl.ds(z + 2, PB)] - b * fz
+        fy = NEAR * (at(0, r + 1, e + 1) - p) - (at(0, r + 2, e + 2) - at(0, r - 1, e - 1))
+        new_y = VY[zs, r:e, :] - b * fy
+        fx = NEAR * (pltpu.roll(p, 127, 2) - p) - (pltpu.roll(p, 126, 2) - pltpu.roll(p, 1, 2))
+        new_x = VX[zs] - b * (fx + HP[...])
+        outside = []
+        for y0 in (PAD - 8, PAD + CY):
+            y1 = y0 + 8
+            f = NEAR * (at(0, y0 + 1, y1 + 1) - at(0, y0, y1)) - (
+                at(0, y0 + 2, y1 + 2) - at(0, y0 - 1, y1 - 1)
             )
-
-        XO[0, z] = XO[0, z] - XO[1, z] * jnp.where(from_low, along(low), along(high))
-        for y0 in (PAD - 8, PAD + CY):
-            f = C1 * (P_[s, z + 1, y0 + 1 : y0 + 9, :] - P_[s, z + 1, y0 : y0 + 8, :]) - C2 * (
-                P_[s, z + 1, y0 + 2 : y0 + 10, :] - P_[s, z + 1, y0 - 1 : y0 + 7, :]
-            )
-            VY[z, y0 : y0 + 8, :] = VY[z, y0 : y0 + 8, :] - B[z, y0 : y0 + 8, :] * f
-        for y0 in range(0, CY, CHUNK):
-            r = PAD + y0
-            e = r + CHUNK
-            p = P_[s, z + 1, r:e, :]
-            b = B[z, r:e, :]
-            halo = jnp.concatenate(
-                [pltpu.roll(near, unroll_shift(y0 // 8 + i), 1) for i in range(CHUNK // 8)], axis=0
-            )
-            left = jnp.where(wide == 127, halo, p)
-            next_ = jnp.where(wide == 0, halo, p)
-            after = jnp.where(wide < 2, halo, p)
-            f = C1 * (pltpu.roll(next_, 127, 1) - p) - C2 * (
-                pltpu.roll(after, 126, 1) - pltpu.roll(left, 1, 1)
-            )
-            VX[z, y0 : y0 + CHUNK, :] = VX[z, y0 : y0 + CHUNK, :] - b * f
-            f = C1 * (P_[s, z + 1, r + 1 : e + 1, :] - p) - C2 * (
-                P_[s, z + 1, r + 2 : e + 2, :] - P_[s, z + 1, r - 1 : e - 1, :]
-            )
-            VY[z, r:e, :] = VY[z, r:e, :] - b * f
-            f = C1 * (P_[s, z + 2, r:e, :] - p) - C2 * (P_[s, z + 3, r:e, :] - P_[s, z, r:e, :])
-            VZ[s + 1, z + 2, y0 : y0 + CHUNK, :] = VZ[s, z + 2, y0 : y0 + CHUNK, :] - b * f
-
-    def pressures(s, z):
-        near = XO[0, z]
-        packed = jnp.zeros((8, 128), F32)
-        for y0 in range(0, CY, CHUNK):
-            r = PAD + y0
-            e = r + CHUNK
-            halo = jnp.concatenate(
-                [pltpu.roll(near, unroll_shift(y0 // 8 + i), 1) for i in range(CHUNK // 8)], axis=0
-            )
-            v = VX[z, y0 : y0 + CHUNK, :]
-            left = jnp.where(wide == 127, halo, v)
-            before = jnp.where(wide >= 126, halo, v)
-            next_ = jnp.where(wide == 0, halo, v)
-            div = C1 * (v - pltpu.roll(left, 1, 1)) - C2 * (
-                pltpu.roll(next_, 127, 1) - pltpu.roll(before, 2, 1)
-            )
-            div = div + (
-                C1 * (VY[z, r:e, :] - VY[z, r - 1 : e - 1, :])
-                - C2 * (VY[z, r + 1 : e + 1, :] - VY[z, r - 2 : e - 2, :])
-            )
-            q, t = y0, y0 + CHUNK
-            div = div + (
-                C1 * (VZ[s + 1, z + 2, q:t, :] - VZ[s + 1, z + 1, q:t, :])
-                - C2 * (VZ[s + 1, z + 3, q:t, :] - VZ[s + 1, z, q:t, :])
-            )
-            one = RELAX1 * M1[z, q:t, :] + FEED1 * div
-            two = RELAX2 * M2[z, q:t, :] + FEED2 * div
-            M1[z, q:t, :] = one
-            M2[z, q:t, :] = two
-            new = P_[s, z + 1, r:e, :] - MOD[z, q:t, :] * (div - one - two) + SRC[s, z, q:t, :]
-            P_[s + 1, z + 1, r:e, :] = new
-            for i in range(CHUNK // 8):
-                block = y0 // 8 + i
-                rolled = pltpu.roll(new[8 * i : 8 * i + 8, :], (8 * block + 3) % 128, 1)
-                packed = jnp.where(group == block, rolled, packed)
-        PO[s + 1, z] = packed
+            outside.append((y0, VY[zs, y0:y1, :] - B[zs, y0:y1, :] * f))
+        VZ[s + 1, pl.ds(z + 2, PB)] = new_z
+        VY[zs, r:e, :] = new_y
+        VX[zs] = new_x
+        for y0, value in outside:
+            VY[zs, y0 : y0 + 8, :] = value
+
+    def pressures(s, k):
+        z = k * PB
+        zs = pl.ds(z, PB)
+        r, e = PAD, PAD + CY
+        v = VX[zs]
+        div = NEAR * (v - pltpu.roll(v, 1, 2)) - (pltpu.roll(v, 127, 2) - pltpu.roll(v, 2, 2))
+        div = div + HV[k % 2]
+        div = div + (
+            NEAR * (VY[zs, r:e, :] - VY[zs, r - 1 : e - 1, :])
+            - (VY[zs, r + 1 : e + 1, :] - VY[zs, r - 2 : e - 2, :])
+        )
+
+        def at(dz):
+            return VZ[s + 1, pl.ds(z + 2 + dz, PB)]
+
+        div = div + (NEAR * (at(0) - at(-1)) - (at(1) - at(-2)))
+        one = RELAX1 * M1[zs] + (FEED1 * UNIT) * div
+        two = RELAX2 * M2[zs] + (FEED2 * UNIT) * div
+        new = P_[s, pl.ds(z + 1, PB), r:e, :] - MOD[zs] * (UNIT * div - one - two) + SRC[s, zs]
+        M1[zs] = one
+        M2[zs] = two
+        P_[s + 1, pl.ds(z + 1, PB), r:e, :] = new
+        for i in range(PB):
+            PO[s + 1, z + i] = pack_rows(lambda q: new[i, 8 * q : 8 * q + 8, :], group)
 
     def stores(g):
         zs = pl.ds(g * GZ, GZ)
         pairs = [
             (P_.at[STEPS, pl.ds(g * GZ + 1, GZ), pl.ds(PAD, CY), :], p_out.at[zs]),
-            (VX.at[zs], vx_out.at[zs]),
             (VY.at[zs, pl.ds(PAD, CY), :], vy_out.at[zs]),
             (VZ.at[STEPS, pl.ds(g * GZ + 2, GZ)], vz_out.at[zs]),
-            (M1.at[zs], m1_out.at[zs]),
-            (M2.at[zs], m2_out.at[zs]),
         ]
         return [pltpu.make_async_copy(a, b, st_sem.at[g, i]) for i, (a, b) in enumerate(pairs)]
 
     def step(s, carry):
-        def planes(z, inner_carry):
-            @pl.when(z < NZ)
+        def planes(k, inner_carry):
+            @pl.when(k < NZ // PB)
             def _():
-                @pl.when(z % GZ == 0)
+                @pl.when(k % (GZ // PB) == 0)
                 def _():
-                    wait_rims(s, z // GZ)
-
-                velocities(s, z)
-
-            @pl.when(z > 0)
+                    wait_rims(s, k // (GZ // PB))
+
+                rims(s, k)
+                velocities(s, k)
+
+            @pl.when(k > 0)
             def _():
-                pressures(s, z - 1)
-
-                @pl.when(z % GZ == 0)
+                pressures(s, k - 1)
+
+                @pl.when(k % (GZ // PB) == 0)
                 def _():
-                    g = z // GZ - 1
+                    g = k // (GZ // PB) - 1
 
                     @pl.when(s < STEPS - 1)
                     def _():
@@ -502,7 +508,7 @@
 
             return inner_carry
 
-        return lax.fori_loop(0, NZ + 1, planes, carry)
+        return lax.fori_loop(0, NZ // PB + 1, planes, carry)
 
     lax.fori_loop(0, STEPS, step, 0)
 
@@ -542,8 +548,8 @@
         both = jnp.concatenate([cosine * real + sine * imag, cosine * imag - sine * real], axis=1)
         high, low = split2(both)
         total = total + (dot(hot[:, t0:t1], high) + dot(hot[:, t0:t1], low))
-    for j in range(ny):
-        RA[ny + j] = total[j * nx : (j + 1) * nx, :]
+    for j in range(outer):
+        RA[outer + j] = total[j * inner : (j + 1) * inner, :]
 
     def exchange(targets, source_of, slots, send, recv):
         copies = []
@@ -560,18 +566,14 @@
             copies.append(copy)
         return copies
 
-    copies = exchange(peers_a, lambda k: RA.at[ny + (gy + k) % ny], RA, sa, ra)
-    part = RA[ny + gy]
+    def block_of(a, b):
+        return (gy + a) % ny * XOUT + (xo + b) % XOUT
+
+    copies = exchange(peers_a, lambda k: RA.at[outer + block_of(*offsets[k - 1])], RA, sa, ra)
+    part = RA[outer + block_of(0, 0)]
     for k, copy in enumerate(copies):
         copy.wait()
         part = part + RA[k + 1]
-    for j in range(XOUT):
-        RB[XOUT + j] = part[j * inner : (j + 1) * inner, :]
-    copies = exchange(peers_b, lambda k: RB.at[XOUT + (xo + k) % XOUT], RB, sb, rb)
-    part = RB[XOUT + xo]
-    for k, copy in enumerate(copies):
-        copy.wait()
-        part = part + RB[k + 1]
     RC[0] = part
     copies = exchange(peers_c, lambda k: RC.at[0], RC, sc, rc)
     for k, copy in enumerate(copies):
@@ -619,29 +621,46 @@
     return high, low
 
 
+def edge_weights():
+    forward = np.zeros((8, CX), np.float32)
+    for place in (0, 2, 5):
+        forward[place, 0] = 1.0
+    for place in (1, 3, 6):
+        forward[place, CX - 1] = NEAR
+        forward[place, CX - 2] = -1.0
+    for place in (4, 7):
+        forward[place, CX - 1] = -1.0
+    backward = np.zeros((8, CX), np.float32)
+    for place in (1, 4):
+        backward[place, 0] = 1.0
+    for place in (0, 2, 5):
+        backward[place, 0] = -NEAR
+        backward[place, 1] = 1.0
+    for place in (3, 6):
+        backward[place, CX - 1] = -1.0
+    return [np.tile(w, (16, 1)).astype(jnp.bfloat16) for w in (forward, backward)]
+
+
 def local(nx, ny, *args):
     fields = args[:8]
     tile_row, tile_owner, src_cell, src_wave = args[8:]
     rows = tile_row.reshape(TILES)
     high, low = tables()
-    block = jax.ShapeDtypeStruct((NZ, CY, CX), F32)
     anywhere = pl.BlockSpec(memory_space=pl.ANY)
     vmem = pl.BlockSpec(memory_space=pltpu.VMEM)
     smem = pl.BlockSpec(memory_space=pltpu.SMEM)
     dma = pltpu.SemaphoreType.DMA
     inner = nx // XOUT
+    outer = ny * XOUT
     return pl.pallas_call(
         functools.partial(kernel, nx, ny),
-        out_shape=[block] * 6 + [jax.ShapeDtypeStruct((2, ANG), F32)],
-        in_specs=[anywhere] * 8 + [smem] + [vmem] * 6,
-        out_specs=[anywhere] * 6 + [vmem],
+        out_shape=[pltpu.VMEM((NZ, CY, CX), F32)] * 6 + [jax.ShapeDtypeStruct((2, ANG), F32)],
+        in_specs=[anywhere] * 8 + [smem] + [vmem] * 8,
+        out_specs=[vmem] * 7,
         scratch_shapes=[
             pltpu.VMEM((STEPS + 1, NZ + 3, ROWS, CX), F32),
-            pltpu.VMEM((NZ, CY, CX), F32),
             pltpu.VMEM((NZ, ROWS, CX), F32),
             pltpu.VMEM((STEPS + 1, NZ + 3, CY, CX), F32),
-            pltpu.VMEM((NZ, CY, CX), F32),
-            pltpu.VMEM((NZ, CY, CX), F32),
             pltpu.VMEM((NZ, ROWS, CX), F32),
             pltpu.VMEM((NZ, CY, CX), F32),
             pltpu.VMEM((NZ, CY, CX), F32),
@@ -649,23 +668,23 @@
             pltpu.VMEM((STEPS + 1, NZ, 8, CX), F32),
             pltpu.VMEM((STEPS, 2, NZ, 8, CX), F32),
             pltpu.VMEM((2, NZ, 8, CX), F32),
+            pltpu.VMEM((2, NZ, 8, CX), F32),
             pltpu.VMEM((2, 2, NZ, 8, CX), F32),
             pltpu.VMEM((3, TILES, ANG), F32),
             pltpu.VMEM((3, STEPS * CX, SRCS), BF16),
+            pltpu.VMEM((PB, CY, CX), F32),
+            pltpu.VMEM((2, PB, CY, CX), F32),
             pltpu.VMEM((2 * STEPS, TILES, CX), F32),
-            pltpu.VMEM((2 * ny, nx, 2 * ANG), F32),
-            pltpu.VMEM((2 * XOUT, inner, 2 * ANG), F32),
+            pltpu.VMEM((2 * outer, inner, 2 * ANG), F32),
             pltpu.VMEM((inner, inner, 2 * ANG), F32),
             dma((8,)),
-            dma((NG, 6)),
+            dma((NG, 3)),
             dma((STEPS, NG, 4)),
             dma((STEPS, NG, 4)),
             dma((4, 2)),
             dma((4, 2)),
-            dma((ny - 1,)),
-            dma((ny - 1,)),
-            dma((XOUT - 1,)),
-            dma((XOUT - 1,)),
+            dma((outer - 1,)),
+            dma((outer - 1,)),
             dma((inner - 1,)),
             dma((inner - 1,)),
         ],
@@ -681,6 +700,7 @@
         src_wave.reshape(STEPS, SRCS),
         high,
         low,
+        *edge_weights(),
     )
 
 

time: 78 us -> 63.1 us (0.81); the launches traced: 77 us -> 63 us
  Pallas kernels: 66 us -> 55.9 us
  local copies, waits for them, and re-layouts: 10.3 us -> 6.39 us
    pallas_call x1, Pallas kernels: 66 us -> 55.9 us  [local(): pl.pallas_call(functools.partial(kernel, nx, ny), out_shape=[pltpu.VMEM((...]
    unnamed x19 -> x9, local copies, waits for them, and re-layouts: 10.3 us -> 6.39 us
where the time goes in v1:
time: 63.1 us; the launch traced here: 63 us
  Pallas kernels  55.9 us (89%)
  local copies, waits for them, and re-layouts  6.39 us (10%)
  between operations  0.65 us (1%)
    pallas_call x1, Pallas kernels, local(): pl.pallas_call(functools.partial(kernel, nx, ny), out_shape=[pltpu.VMEM((...  55.9 us
    unnamed x9, local copies, waits for them, and re-layouts  6.39 us

profile of v1, /device:TPU:1, one launch (start us, length us, event | category | flops | bytes accessed | tf_op | source)
XLA Modules:
  0.0 63.0 jit_solution(11831232646012341563)
XLA Ops:
  0.6 55.9 %shard_map.207 = (f32[16,128,128]{2,1,0:T(8,128)S(1)}, f32[16,128,128]{2,1,0:T(8,128)S(1)}, f32[16,128,128]{2,1,0:T(8,128)S(1)}, f32[16,128,128]{2,1,0:T(8,128)S...) custom-call(f32[16,128,128]{2,1,0:T(8,128)} %p_in.1, f32[16,128,128]{2,1,0:T(8,128)} %vx_in.1, ...), custom_call_target="tpu_custom_call" | custom-call | tf_op jit(solution)/shard_map/pallas_call | solution.py:655
  56.6 1.0 %copy.30 = f32[16,128,128]{2,1,0:T(8,128)} copy(f32[16,128,128]{2,1,0:T(8,128)S(1)} %get-tuple-element.7) | data formatting | bytes 2097152
  57.5 1.0 %copy.31 = f32[16,128,128]{2,1,0:T(8,128)} copy(f32[16,128,128]{2,1,0:T(8,128)S(1)} %get-tuple-element.8) | data formatting | bytes 2097152
  58.5 1.0 %copy.32 = f32[16,128,128]{2,1,0:T(8,128)} copy(f32[16,128,128]{2,1,0:T(8,128)S(1)} %get-tuple-element.9) | data formatting | bytes 2097152
  59.5 1.0 %copy.33 = f32[16,128,128]{2,1,0:T(8,128)} copy(f32[16,128,128]{2,1,0:T(8,128)S(1)} %get-tuple-element.10) | data formatting | bytes 2097152
  60.5 1.0 %copy.34 = f32[16,128,128]{2,1,0:T(8,128)} copy(f32[16,128,128]{2,1,0:T(8,128)S(1)} %get-tuple-element.11) | data formatting | bytes 2097152
  61.4 0.0 copy-start
  61.4 1.0 %copy.35 = f32[16,128,128]{2,1,0:T(8,128)} copy(f32[16,128,128]{2,1,0:T(8,128)S(1)} %get-tuple-element.12) | data formatting | bytes 2097152
  62.4 0.0 copy-done
  62.4 0.6 copy.36
Async XLA Ops:
  61.4 1.0 %copy-start = (f32[2,128]{1,0:T(2,128)S(1)}, f32[2,128]{1,0:T(2,128)}, u32[]{:S(2)}) copy-start(f32[2,128]{1,0:T(2,128)} %get-tuple-element.27) | copy-start | bytes 3076

commit v2 on v1

--- a/solution.py
+++ b/solution.py
@@ -186,9 +186,9 @@
             source = PO.at[s, pl.ds(z0, GZ)]
             target = PH.at[s, HIGH_X if d == LOW_X else LOW_X, pl.ds(z0, GZ)]
         else:
-            y_from, y_to = (PAD, PAD + CY) if d == LOW_Y else (PAD + CY - 8, PAD - 8)
-            source = P_.at[s, pl.ds(z0 + 1, GZ), pl.ds(y_from, 8), :]
-            target = P_.at[s, pl.ds(z0 + 1, GZ), pl.ds(y_to, 8), :]
+            y_from, y_to = (PAD, PAD + CY) if d == LOW_Y else (PAD + CY - 4, PAD - 4)
+            source = P_.at[s, pl.ds(z0 + 1, GZ), pl.ds(y_from, 4), :]
+            target = P_.at[s, pl.ds(z0 + 1, GZ), pl.ds(y_to, 4), :]
         back = {LOW_X: HIGH_X, HIGH_X: LOW_X, LOW_Y: HIGH_Y, HIGH_Y: LOW_Y}[d]
         return pltpu.make_async_remote_copy(
             src_ref=source,
@@ -219,10 +219,10 @@
         if d in (LOW_X, HIGH_X):
             pairs = [(XO, XH.at[back])]
         else:
-            y_from, y_to = (0, PAD + CY) if d == LOW_Y else (CY - 8, PAD - 8)
+            y_from, y_to = (0, PAD + CY) if d == LOW_Y else (CY - 4, PAD - 4)
             pairs = [
-                (vy_in.at[:, pl.ds(y_from, 8), :], VY.at[:, pl.ds(y_to, 8), :]),
-                (de_in.at[:, pl.ds(y_from, 8), :], B.at[:, pl.ds(y_to, 8), :]),
+                (vy_in.at[:, pl.ds(y_from, 4), :], VY.at[:, pl.ds(y_to, 4), :]),
+                (de_in.at[:, pl.ds(y_from, 4), :], B.at[:, pl.ds(y_to, 4), :]),
             ]
         return [
             pltpu.make_async_remote_copy(
@@ -521,7 +521,7 @@
             G[STEPS + s, pl.ds(t, 1), :] = VZ[s + 1, z + 2, pl.ds(y, 1), :]
         return carry
 
-    lax.fori_loop(0, TILES, gather, 0, unroll=8)
+    lax.fori_loop(0, TILES, gather, 0, unroll=32)
 
     weights = [(math.cos(STEP_PHASE * (s + 1)), math.sin(STEP_PHASE * (s + 1))) for s in range(STEPS)]
     own_row = own_v[...]

time: 63.1 us -> 62.7 us (level)
  no operation moved by 1% of the time
where the time goes in v2:
time: 62.7 us; the launch traced here: 62.6 us
  Pallas kernels  55.6 us (89%)
  local copies, waits for them, and re-layouts  6.39 us (10%)
  between operations  0.65 us (1%)
    pallas_call x1, Pallas kernels, local(): pl.pallas_call(functools.partial(kernel, nx, ny), out_shape=[pltpu.VMEM((...  55.6 us
    unnamed x9, local copies, waits for them, and re-layouts  6.39 us

profile of v2, /device:TPU:1, one launch (start us, length us, event | category | flops | bytes accessed | tf_op | source)
XLA Modules:
  0.0 62.6 jit_solution(9553493571019794174)
XLA Ops:
  0.6 55.6 %shard_map.207 = (f32[16,128,128]{2,1,0:T(8,128)S(1)}, f32[16,128,128]{2,1,0:T(8,128)S(1)}, f32[16,128,128]{2,1,0:T(8,128)S(1)}, f32[16,128,128]{2,1,0:T(8,128)S...) custom-call(f32[16,128,128]{2,1,0:T(8,128)} %p_in.1, f32[16,128,128]{2,1,0:T(8,128)} %vx_in.1, ...), custom_call_target="tpu_custom_call" | custom-call | tf_op jit(solution)/shard_map/pallas_call | solution.py:655
  56.2 1.0 %copy.30 = f32[16,128,128]{2,1,0:T(8,128)} copy(f32[16,128,128]{2,1,0:T(8,128)S(1)} %get-tuple-element.7) | data formatting | bytes 2097152
  57.2 1.0 %copy.31 = f32[16,128,128]{2,1,0:T(8,128)} copy(f32[16,128,128]{2,1,0:T(8,128)S(1)} %get-tuple-element.8) | data formatting | bytes 2097152
  58.1 1.0 %copy.32 = f32[16,128,128]{2,1,0:T(8,128)} copy(f32[16,128,128]{2,1,0:T(8,128)S(1)} %get-tuple-element.9) | data formatting | bytes 2097152
  59.1 1.0 %copy.33 = f32[16,128,128]{2,1,0:T(8,128)} copy(f32[16,128,128]{2,1,0:T(8,128)S(1)} %get-tuple-element.10) | data formatting | bytes 2097152
  60.1 1.0 %copy.34 = f32[16,128,128]{2,1,0:T(8,128)} copy(f32[16,128,128]{2,1,0:T(8,128)S(1)} %get-tuple-element.11) | data formatting | bytes 2097152
  61.1 0.0 copy-start
  61.1 1.0 %copy.35 = f32[16,128,128]{2,1,0:T(8,128)} copy(f32[16,128,128]{2,1,0:T(8,128)S(1)} %get-tuple-element.12) | data formatting | bytes 2097152
  62.0 0.0 copy-done
  62.0 0.6 copy.36
Async XLA Ops:
  61.1 1.0 %copy-start = (f32[2,128]{1,0:T(2,128)S(1)}, f32[2,128]{1,0:T(2,128)}, u32[]{:S(2)}) copy-start(f32[2,128]{1,0:T(2,128)} %get-tuple-element.27) | copy-start | bytes 3076
